TPU v7x, 256 devices: a whole 4x4x8 slice. The times are simulated.
256 devices in a mesh: trow: 16 (over x, y), tcol: 8 (over z), rep: 2 (over core).
Axes of the slice: x: 4, y: 4, z: 8, core: 2. Of those that a mesh axis runs over, the one named last changes fastest.
Arguments:
- users: float32 [131072, 128], P(('trow', 'tcol'))
- items: float32 [65536, 128], P(('tcol', 'trow'))
- ratings: bfloat16 [16, 8, 2, 64, 128, 128], P('trow', 'tcol', 'rep'), may hold values from -6 to 6
- row_mask: int32 [16, 8, 2, 64, 128], P('trow', 'tcol', 'rep'), may hold values 0 or 1
- col_mask: int32 [16, 8, 2, 64, 128], P('trow', 'tcol', 'rep'), may hold values 0 or 1
- row_slots: int32 [16, 8, 2, 64], P('trow', 'tcol', 'rep'), may hold values from 0 to 31, as said below
- col_slots: int32 [16, 8, 2, 64], P('trow', 'tcol', 'rep'), may hold values from 0 to 31, as said below
- send_users: int32 [16, 8, 2, 8, 4], P('trow', 'tcol', 'rep'), may hold values from 0 to 7, as said below
- send_items: int32 [16, 8, 2, 16, 2], P('trow', 'tcol', 'rep'), may hold values from 0 to 3, as said below
Outputs:
- users_out: float32 [131072, 128], P(('trow', 'tcol'))
- items_out: float32 [65536, 128], P(('tcol', 'trow'))
Inputs may be any that keep to these rules, and one draw needn't show every extreme that they name: `send_users`: distinct within each row of the last dimension. `send_items`: distinct within each row of the last dimension. `row_slots`: every slot is named by some tile of each device. `col_slots`: every slot is named by some tile of each device.
All inputs are finite; a program needn't handle non-finite values. No bound on the sum of `row_mask` or of `col_mask` on one device may be relied on, other than what follows from the above.
Results may differ from a plain program's by a relative error of at most 0.02.
Values may be sent and summed in bfloat16 or wider, within the bound.
A program may use at most 64 MiB of HBM per device.

v0:
```python
import jax
import jax.numpy as jnp
from jax import lax
from jax.sharding import PartitionSpec as P

ITERS = 2


def precondition(gradient, gramian):
    factor = jnp.linalg.cholesky(gramian)
    return jax.scipy.linalg.cho_solve((factor, True), gradient.T).T


def pool_sum(index_list, terms, pool_count):
    onehot = (
        lax.broadcasted_iota(jnp.int32, (pool_count, index_list.shape[0]), 0) == index_list[None, :]
    ).astype(jnp.bfloat16)
    flat = terms.reshape(terms.shape[0], -1)
    upper = flat.astype(jnp.bfloat16)
    lower = (flat - upper.astype(jnp.float32)).astype(jnp.bfloat16)
    return jnp.dot(onehot, upper, preferred_element_type=jnp.float32) + jnp.dot(
        onehot, lower, preferred_element_type=jnp.float32
    )


def on_device(
    users, items, ratings, row_mask, col_mask, row_slots, col_slots, send_users, send_items
):
    n_trow = lax.axis_size("trow")
    n_tcol = lax.axis_size("tcol")
    n_rep = lax.axis_size("rep")
    tile_size = ratings.shape[-1]
    rank_width = users.shape[1]
    tile_count = ratings.shape[3]
    own_users = users.shape[0] // tile_size
    own_items = items.shape[0] // tile_size
    user_cap = send_users.shape[-1]
    item_cap = send_items.shape[-1]
    ratings_local = ratings.reshape(tile_count, tile_size, tile_size)
    weights = (
        row_mask.reshape(tile_count, tile_size)[:, :, None]
        * col_mask.reshape(tile_count, tile_size)[:, None, :]
    ).astype(jnp.float32)
    row_slot_list = row_slots.reshape(-1)
    col_slot_list = col_slots.reshape(-1)
    user_sends = send_users.reshape(n_tcol, -1)
    item_sends = send_items.reshape(n_trow, -1)
    user_received = lax.all_to_all(
        user_sends, "tcol", split_axis=0, concat_axis=0, tiled=True
    ).reshape(-1)
    item_received = lax.all_to_all(
        item_sends, "trow", split_axis=0, concat_axis=0, tiled=True
    ).reshape(-1)
    row_list = row_slot_list // user_cap * own_users + user_received[row_slot_list]
    col_list = col_slot_list // item_cap * own_items + item_received[col_slot_list]
    all_users = own_users * tile_size * n_trow * n_tcol
    all_items = own_items * tile_size * n_trow * n_tcol
    user_coef = 2.0 * all_items * own_users / (tile_size * tile_count * n_rep)
    item_coef = 2.0 * all_users * own_items / (tile_size * tile_count * n_rep)
    for iteration in range(ITERS):
        gram_users, gram_items = lax.psum(
            (
                jnp.dot(
                    users.T,
                    users,
                    precision=lax.Precision.HIGHEST,
                    preferred_element_type=jnp.float32,
                ),
                jnp.dot(
                    items.T,
                    items,
                    precision=lax.Precision.HIGHEST,
                    preferred_element_type=jnp.float32,
                ),
            ),
            ("trow", "tcol"),
        )
        user_half = users.astype(jnp.bfloat16).reshape(own_users, tile_size, rank_width)
        item_half = items.astype(jnp.bfloat16).reshape(own_items, tile_size, rank_width)
        user_pool = lax.all_gather(user_half, "tcol", axis=0, tiled=True)
        item_pool = lax.all_gather(item_half, "trow", axis=0, tiled=True)
        x_tiles = user_pool[row_list]
        y_tiles = item_pool[col_list]
        predicted = jnp.einsum("tar,tbr->tab", x_tiles, y_tiles, preferred_element_type=jnp.float32)
        errors = (weights * (predicted - ratings_local.astype(jnp.float32))).astype(jnp.bfloat16)
        user_terms = jnp.einsum("tab,tbr->tar", errors, y_tiles, preferred_element_type=jnp.float32)
        item_terms = jnp.einsum("tab,tar->tbr", errors, x_tiles, preferred_element_type=jnp.float32)
        user_pooled = pool_sum(row_list, user_terms, user_pool.shape[0])
        item_pooled = pool_sum(col_list, item_terms, item_pool.shape[0])
        user_grad = lax.psum_scatter(user_pooled, "tcol", scatter_dimension=0, tiled=True)
        item_grad = lax.psum_scatter(item_pooled, "trow", scatter_dimension=0, tiled=True)
        user_grad, item_grad = lax.psum((user_grad, item_grad), "rep")
        new_users = users - user_coef * precondition(user_grad.reshape(-1, rank_width), gram_items)
        new_items = items - item_coef * precondition(item_grad.reshape(-1, rank_width), gram_users)
        users, items = (new_users, new_items)
    return (users, items)


def solution(mesh):
    return jax.shard_map(
        on_device,
        mesh=mesh,
        in_specs=(
            P(("trow", "tcol"), None),
            P(("tcol", "trow"), None),
            P("trow", "tcol", "rep", None, None, None),
            P("trow", "tcol", "rep", None, None),
            P("trow", "tcol", "rep", None, None),
            P("trow", "tcol", "rep", None),
            P("trow", "tcol", "rep", None),
            P("trow", "tcol", "rep", None, None),
            P("trow", "tcol", "rep", None, None),
        ),
        out_specs=(P(("trow", "tcol"), None), P(("tcol", "trow"), None)),
        check_vma=False,
    )
```

profile of v0, /device:TPU:1, one launch (start us, length us, event | category | flops | bytes accessed | tf_op | source)
XLA Modules:
  0.0 1075.5 jit_solution(2654260133140196737)
XLA Ops:
  7.2 1.8 convert_element_type.69
  9.1 1.6 convert_element_type.70
  10.7 1.3 copy.48
  12.1 7.6 all-to-all-start.1
  21.0 1.3 copy.47
  22.3 3.7 all-to-all-done.1
  26.1 8.2 all-to-all-start
  36.4 4.4 all-to-all-done
  42.3 9.4 all-gather.5.cloned.1.call-done
  51.7 3.7 gather_fusion.1
  55.4 50.8 %all-gather.7.cloned.1.call-done = bf16[64,128,128]{2,1,0:T(8,128)(2,1)} async-done(((bf16[4,128,128]{2,1,0:T(8,128)(2,1)}), bf16[64,128,128]{2,1,0:T(8,128)(2,1)}) %all-gather.7.cloned.1.call-update) | async-done | bytes 2097168 | tf_op jit(solution)/shard_map/all_gather | solution.py:81
  106.3 2.5 gather_fusion.3
  108.9 4.1 fusion.1
  113.0 0.9 fusion.61
  114.4 2.8 fusion.9
  117.2 4.9 convolution_add_fusion.2
  122.3 2.3 fusion.59
  124.6 2.8 fusion.8
  127.4 4.9 convolution_add_fusion.3
  132.4 0.9 copy-done.5
  133.2 1.2 fusion.58
  134.5 1.6 fusion.60
  137.4 98.5 %all-reduce.13.cloned.1.call-done = f32[64,16384]{1,0:T(8,128)} async-done(((f32[64,16384]{1,0:T(8,128)}), f32[64,16384]{1,0:T(8,128)}) %all-reduce.13.cloned.1.call-update) | async-done | bytes 4194320
  235.9 1.1 constant_dynamic-slice_fusion.1
  237.0 0.9 reshape.383
  237.9 55.8 %reduce-scatter.3.cloned.1.call-done = f32[8,16384]{1,0:T(8,128)} async-done(((f32[64,16384]{1,0:T(8,128)}), f32[8,16384]{1,0:T(8,128)}) %reduce-scatter.3.cloned.1.call-update) | async-done | bytes 524304 | tf_op jit(solution)/shard_map/reduce_scatter | solution.py:90
  293.7 1.9 reshape.380
  296.1 209.1 %all-reduce.19.cloned.1.call-done = (f32[128,128]{0,1:T(8,128)}, f32[128,128]{0,1:T(8,128)}) async-done(((f32[128,128]{0,1:T(8,128)}, f32[128,128]{0,1:T(8,128)}), (f32[128,128]{0,1:T(8,128)}, f32[128,128]{0,1:T(8,128)})) %all-reduce.19.cloned.1.call-update) | async-done | bytes 131088 | tf_op jit(solution)/shard_map/psum | solution.py:61
  505.3 0.9 copy.51
  506.2 0.9 copy.46
  507.1 0.9 fusion.39
  508.0 11.7 %cholesky.74 = f32[128,128]{1,0:T(8,128)S(1)} custom-call(f32[128,128]{1,0:T(8,128)S(1)} %get-tuple-element.24), custom_call_target="Cholesky" | custom-call | tf_op jit(solution)/shard_map/jit(cholesky)/cholesky | solution.py:10
  521.1 9.8 custom-call.14
  530.9 10.3 all-reduce.23.cloned.1.call-done
  541.2 1.7 fusion.41
  545.1 11.7 %cholesky.85 = f32[128,128]{1,0:T(8,128)S(1)} custom-call(f32[128,128]{1,0:T(8,128)S(1)} %get-tuple-element.23), custom_call_target="Cholesky" | custom-call | tf_op jit(solution)/shard_map/jit(cholesky)/cholesky | solution.py:10
  558.1 9.8 custom-call.15
  569.6 1.0 fusion.62
  570.6 1.2 fusion.64
  572.0 10.9 %all-gather.9.cloned.1.call-done = bf16[64,128,128]{2,1,0:T(8,128)(2,1)} async-done(((bf16[8,128,128]{2,1,0:T(8,128)(2,1)}), bf16[64,128,128]{2,1,0:T(8,128)(2,1)}) %all-gather.9.cloned.1.call-update) | async-done | bytes 2097168 | tf_op jit(solution)/shard_map/all_gather | solution.py:80
  582.9 3.7 gather_fusion.4
  586.7 50.5 %all-gather.11.cloned.1.call-done = bf16[64,128,128]{2,1,0:T(8,128)(2,1)} async-done(((bf16[4,128,128]{2,1,0:T(8,128)(2,1)}), bf16[64,128,128]{2,1,0:T(8,128)(2,1)}) %all-gather.11.cloned.1.call-update) | async-done | bytes 2097168 | tf_op jit(solution)/shard_map/all_gather | solution.py:81
  637.2 2.5 gather_fusion.5
  639.7 4.1 fusion.3
  643.9 0.9 fusion.65
  645.2 2.8 fusion.11
  648.0 4.9 convolution_add_fusion
  653.0 2.3 fusion.63
  655.3 2.8 fusion.10
  658.1 4.9 convolution_add_fusion.1
  663.2 187.3 %all-reduce.17.cloned.1.call-done = (f32[128,128]{0,1:T(8,128)}, f32[128,128]{0,1:T(8,128)}) async-done(((f32[128,128]{0,1:T(8,128)}, f32[128,128]{0,1:T(8,128)}), (f32[128,128]{0,1:T(8,128)}, f32[128,128]{0,1:T(8,128)})) %all-reduce.17.cloned.1.call-update) | async-done | bytes 131088 | tf_op jit(solution)/shard_map/psum | solution.py:61
  850.6 1.0 copy.55
  851.5 0.9 fusion.35
  852.4 11.7 %cholesky.96 = f32[128,128]{1,0:T(8,128)S(1)} custom-call(f32[128,128]{1,0:T(8,128)S(1)} %fusion.35), custom_call_target="Cholesky" | custom-call | tf_op jit(solution)/shard_map/jit(cholesky)/cholesky | solution.py:10
  864.8 104.5 %all-reduce.15.cloned.1.call-done = f32[64,16384]{1,0:T(8,128)} async-done(((f32[64,16384]{1,0:T(8,128)}), f32[64,16384]{1,0:T(8,128)}) %all-reduce.15.cloned.1.call-update) | async-done | bytes 4194320
  969.4 1.1 constant_dynamic-slice_fusion
  970.5 0.9 reshape.389
  971.4 56.1 %reduce-scatter.5.cloned.1.call-done = f32[8,16384]{1,0:T(8,128)} async-done(((f32[64,16384]{1,0:T(8,128)}), f32[8,16384]{1,0:T(8,128)}) %reduce-scatter.5.cloned.1.call-update) | async-done | bytes 524304 | tf_op jit(solution)/shard_map/reduce_scatter | solution.py:90
  1027.5 1.9 reshape.387
  1030.1 9.8 custom-call.16
  1040.0 11.7 %cholesky.107 = f32[128,128]{1,0:T(8,128)S(1)} custom-call(f32[128,128]{1,0:T(8,128)S(1)} %fusion.31), custom_call_target="Cholesky" | custom-call | tf_op jit(solution)/shard_map/jit(cholesky)/cholesky | solution.py:10
  1053.2 10.0 custom-call.17
  1063.3 1.7 fusion.33
  1065.6 1.0 copy.61
  (95 shorter events, 19.6 us)
Async XLA Ops:
  7.2 35.1 %copy-start.12 = (s32[1,1,1,64]{3,2,1,0:T(1,128)S(1)}, s32[1,1,1,64]{3,2,1,0:T(1,128)}, u32[]{:S(2)}) copy-start(s32[1,1,1,64]{3,2,1,0:T(1,128)} %param.19) | copy-start | bytes 772
  7.2 29.1 %copy-start.11 = (s32[1,1,1,64]{3,2,1,0:T(1,128)S(1)}, s32[1,1,1,64]{3,2,1,0:T(1,128)}, u32[]{:S(2)}) copy-start(s32[1,1,1,64]{3,2,1,0:T(1,128)} %param.20) | copy-start | bytes 772
  7.2 44.5 %all-gather.5.cloned.1.call-start = ((), (), s32[]{:S(2)}) async-start(), calls=%async_computation.4 | async-start | bytes 2359296 | tf_op jit(solution)/shard_map/all_gather | solution.py:80
  9.0 97.3 %all-gather.7.cloned.1.call-start = ((), (), s32[]{:S(2)}) async-start(), calls=%async_computation.5 | async-start | bytes 2228224 | tf_op jit(solution)/shard_map/all_gather | solution.py:81
  12.1 14.0 %all-to-all-start.1 = ((s32[16,1,2]{2,1,0:T(1,128)}), s32[16,1,2]{2,1,0:T(1,128)S(1)}, u32[]{:S(2)}, u32[]{:S(2)}) async-start(s32[16,1,2]{2,1,0:T(1,128)} %copy.48), calls=%async_computation.1 | async-start | bytes 16384 | tf_op jit(solution)/shard_map/all_to_all | solution.py:51
  26.1 14.7 %all-to-all-start = ((s32[8,1,4]{2,1,0:T(1,128)}), s32[8,1,4]{2,1,0:T(1,128)S(1)}, u32[]{:S(2)}, u32[]{:S(2)}) async-start(s32[8,1,4]{2,1,0:T(1,128)} %copy.47), calls=%async_computation | async-start | bytes 8192 | tf_op jit(solution)/shard_map/all_to_all | solution.py:48
  34.3 201.6 %all-reduce.13.cloned.1.call-start = ((), (), s32[]{:S(2)}) async-start(), calls=%async_computation.10 | async-start | bytes 8388608
  55.4 53.4 %copy-start.9 = (s32[1,1,1,64,128]{4,3,2,1,0:T(8,128)S(1)}, s32[1,1,1,64,128]{4,3,2,1,0:T(8,128)}, u32[]{:S(2)}) copy-start(s32[1,1,1,64,128]{4,3,2,1,0:T(8,128)} %param.18) | copy-start | bytes 98308
  55.4 53.4 %copy-start.10 = (s32[1,1,1,64,128]{4,3,2,1,0:T(8,128)S(1)}, s32[1,1,1,64,128]{4,3,2,1,0:T(8,128)}, u32[]{:S(2)}) copy-start(s32[1,1,1,64,128]{4,3,2,1,0:T(8,128)} %param.17) | copy-start | bytes 98308
  108.9 4.1 copy-start.1
  113.0 1.4 copy-start.2
  122.1 171.6 %reduce-scatter.3.cloned.1.call-start = ((), (), s32[]{:S(2)}) async-start(), calls=%async_computation.6 | async-start | bytes 4718592 | tf_op jit(solution)/shard_map/reduce_scatter | solution.py:90
  132.3 1.0 copy-start.5
  132.3 2.2 copy-start.4
  132.3 3.9 copy-start.13
  132.3 372.9 %all-reduce.19.cloned.1.call-start = ((), (), s32[]{:S(2)}) async-start(), calls=%async_computation.13 | async-start | bytes 262144 | tf_op jit(solution)/shard_map/psum | solution.py:61
  136.1 405.1 %all-reduce.23.cloned.1.call-start = ((), (), s32[]{:S(2)}) async-start(), calls=%async_computation.15 | async-start | bytes 1572864 | tf_op jit(solution)/shard_map/psum | solution.py:92
  295.6 287.3 %all-gather.9.cloned.1.call-start = ((), (), s32[]{:S(2)}) async-start(), calls=%async_computation.7 | async-start | bytes 2359296 | tf_op jit(solution)/shard_map/all_gather | solution.py:80
  541.2 26.7 %copy-start.7 = (f32[128,512]{0,1:T(8,128)S(1)}, f32[128,512]{0,1:T(8,128)}, u32[]{:S(2)}) copy-start(f32[128,512]{0,1:T(8,128)} %get-tuple-element.18) | copy-start | bytes 786436
  544.4 92.8 %all-gather.11.cloned.1.call-start = ((), (), s32[]{:S(2)}) async-start(), calls=%async_computation.8 | async-start | bytes 2228224 | tf_op jit(solution)/shard_map/all_gather | solution.py:81
  569.5 281.0 %all-reduce.17.cloned.1.call-start = ((), (), s32[]{:S(2)}) async-start(), calls=%async_computation.12 | async-start | bytes 262144 | tf_op jit(solution)/shard_map/psum | solution.py:61
  571.8 397.6 %all-reduce.15.cloned.1.call-start = ((), (), s32[]{:S(2)}) async-start(), calls=%async_computation.11 | async-start | bytes 8388608
  639.7 4.1 copy-start
  643.9 1.4 copy-start.3
  652.9 374.5 %reduce-scatter.5.cloned.1.call-start = ((), (), s32[]{:S(2)}) async-start(), calls=%async_computation.9 | async-start | bytes 4718592 | tf_op jit(solution)/shard_map/reduce_scatter | solution.py:90
  663.0 400.3 %all-reduce.21.cloned.1.call-start = ((), (), s32[]{:S(2)}) async-start(), calls=%async_computation.14 | async-start | bytes 1572864 | tf_op jit(solution)/shard_map/psum | solution.py:92
  850.6 189.4 %copy-start.6 = (f32[128,128]{0,1:T(8,128)S(1)}, f32[128,128]{0,1:T(8,128)}, u32[]{:S(2)}) copy-start(f32[128,128]{0,1:T(8,128)} %get-tuple-element.12) | copy-start | bytes 196612
  1063.2 3.3 copy-start.8
Sparse Core Ops, SparseCore 0:
  10.4 41.2 all-gather.4
  54.7 51.5 all-gather.6
  122.2 113.6 all-reduce.12
  238.3 55.3 reduce-scatter.2
  299.1 206.1 all-reduce.18
  508.5 32.6 all-reduce.22
  544.5 38.3 all-gather.8
  585.9 51.1 all-gather.10
  642.7 207.7 all-reduce.16
  854.1 115.2 all-reduce.14
  972.1 55.3 reduce-scatter.4
  1030.7 29.7 all-reduce.20
where the time goes:
time: 1080 us
  waiting for transfers between devices  852 us (79%)
  other arithmetic  99.6 us (9%)
  matrix products  56.4 us (5%)
  local copies, waits for them, and re-layouts  34.4 us (3%)
  starting transfers between devices  17.6 us (2%)
  between operations  15.7 us (1%)
    psum x2, waiting for transfers between devices, on_device(): lax.psum((jnp.dot(users.T, users, precision=lax.Precision.HIGHEST, prefer...  396 us
    unnamed x14, waiting for transfers between devices  203 us
    reduce_scatter x2, waiting for transfers between devices, on_device(): lax.psum_scatter(user_pooled, 'tcol', scatter_dimension=0, tiled=True)  112 us
    all_gather x2, waiting for transfers between devices, on_device(): item_pool = lax.all_gather(item_half, 'trow', axis=0, tiled=True)  101 us
    another operation x12, other arithmetic, precondition(): factor = jnp.linalg.cholesky(gramian)  49.7 us
    another operation x8, other arithmetic, precondition(): return jax.scipy.linalg.cho_solve((factor, True), gradient.T).T  42.1 us
  transfers between devices with their start and end apart: 14, of which 13 were waited for; matrix products, arithmetic and copies ran while one was open for 15% of the time, Pallas kernels for 0%

commit v1 on v0

--- a/solution.py
+++ b/solution.py
@@ -59,21 +59,24 @@
     item_coef = 2.0 * all_users * own_items / (tile_size * tile_count * n_rep)
     for iteration in range(ITERS):
         gram_users, gram_items = lax.psum(
-            (
-                jnp.dot(
-                    users.T,
-                    users,
-                    precision=lax.Precision.HIGHEST,
-                    preferred_element_type=jnp.float32,
+            lax.psum(
+                (
+                    jnp.dot(
+                        users.T,
+                        users,
+                        precision=lax.Precision.HIGHEST,
+                        preferred_element_type=jnp.float32,
+                    ),
+                    jnp.dot(
+                        items.T,
+                        items,
+                        precision=lax.Precision.HIGHEST,
+                        preferred_element_type=jnp.float32,
+                    ),
                 ),
-                jnp.dot(
-                    items.T,
-                    items,
-                    precision=lax.Precision.HIGHEST,
-                    preferred_element_type=jnp.float32,
-                ),
+                "tcol",
             ),
-            ("trow", "tcol"),
+            "trow",
         )
         user_half = users.astype(jnp.bfloat16).reshape(own_users, tile_size, rank_width)
         item_half = items.astype(jnp.bfloat16).reshape(own_items, tile_size, rank_width)

time: 1080 us -> 791 us (0.73)
  waiting for transfers between devices: 852 us -> 562 us
    psum x2, waiting for transfers between devices: 396 us -> 108 us  [on_device(): lax.psum((jnp.dot(users.T, users, precision=lax.Precision.HIGHEST, prefer...]
    psum x0 -> x2, waiting for transfers between devices: none -> 222 us  [on_device(): lax.psum(lax.psum((jnp.dot(users.T, users, precision=lax.Precision.HIGHES...]
    unnamed x14 -> x12, waiting for transfers between devices: 203 us -> 0.2 us
    reduce_scatter x2, waiting for transfers between devices: 112 us -> 97.3 us  [on_device(): lax.psum_scatter(user_pooled, 'tcol', scatter_dimension=0, tiled=True)]
  transfers between devices with their start and end apart: 14 -> 14, of which waited for: 13 -> 13; matrix products, arithmetic and copies ran while one was open for 15% -> 22% of each run, Pallas kernels for 0% -> 0%
where the time goes in v1:
time: 791 us; the launch traced here: 783 us
  waiting for transfers between devices  562 us (71%)
  other arithmetic  97.5 us (12%)
  matrix products  57.4 us (7%)
  local copies, waits for them, and re-layouts  32 us (4%)
  starting transfers between devices  17.6 us (2%)
  between operations  15.8 us (2%)
    psum x2, waiting for transfers between devices, on_device(): lax.psum(lax.psum((jnp.dot(users.T, users, precision=lax.Precision.HIGHES...  222 us
    psum x2, waiting for transfers between devices, on_device(): lax.psum((jnp.dot(users.T, users, precision=lax.Precision.HIGHEST, prefer...  108 us
    all_gather x2, waiting for transfers between devices, on_device(): item_pool = lax.all_gather(item_half, 'trow', axis=0, tiled=True)  101 us
    reduce_scatter x2, waiting for transfers between devices, on_device(): lax.psum_scatter(user_pooled, 'tcol', scatter_dimension=0, tiled=True)  97.3 us
    another operation x12, other arithmetic, precondition(): factor = jnp.linalg.cholesky(gramian)  49.7 us
    another operation x8, other arithmetic, precondition(): return jax.scipy.linalg.cho_solve((factor, True), gradient.T).T  42 us
    all_gather x2, waiting for transfers between devices, on_device(): user_pool = lax.all_gather(user_half, 'tcol', axis=0, tiled=True)  20.2 us
    dot_general x4, matrix products, pool_sum(): jnp.dot(onehot, lower, preferred_element_type=jnp.float32)  19.5 us
  transfers between devices with their start and end apart: 14, of which 13 were waited for; matrix products, arithmetic and copies ran while one was open for 22% of the time, Pallas kernels for 0%

profile of v1, /device:TPU:1, one launch (start us, length us, event | category | flops | bytes accessed | tf_op | source)
XLA Modules:
  0.0 782.7 jit_solution(10044040879026775598)
XLA Ops:
  7.3 1.8 convert_element_type.69
  9.1 1.6 convert_element_type.70
  10.8 1.4 copy.48
  12.1 7.6 all-to-all-start.1
  19.8 2.3 fusion.58
  22.1 1.6 fusion.60
  24.5 1.7 all-to-all-done.1
  26.1 8.2 %all-to-all-start = ((s32[8,1,4]{2,1,0:T(1,128)}), s32[8,1,4]{2,1,0:T(1,128)S(1)}, u32[]{:S(2)}, u32[]{:S(2)}) async-start(s32[8,1,4]{2,1,0:T(1,128)} %copy.47), calls=%async_computation | async-start | bytes 8192 | tf_op jit(solution)/shard_map/all_to_all | solution.py:48
  35.6 0.8 gather_fusion.2
  36.5 4.5 all-to-all-done
  41.7 0.8 gather_fusion
  42.5 9.2 %all-gather.5.cloned.1.call-done = bf16[64,128,128]{2,1,0:T(8,128)(2,1)} async-done(((bf16[8,128,128]{2,1,0:T(8,128)(2,1)}), bf16[64,128,128]{2,1,0:T(8,128)(2,1)}) %all-gather.5.cloned.1.call-update) | async-done | bytes 2097168 | tf_op jit(solution)/shard_map/all_gather | solution.py:83
  51.7 3.8 gather_fusion.1
  55.5 50.7 %all-gather.7.cloned.1.call-done = bf16[64,128,128]{2,1,0:T(8,128)(2,1)} async-done(((bf16[4,128,128]{2,1,0:T(8,128)(2,1)}), bf16[64,128,128]{2,1,0:T(8,128)(2,1)}) %all-gather.7.cloned.1.call-update) | async-done | bytes 2097168 | tf_op jit(solution)/shard_map/all_gather | solution.py:84
  106.2 2.5 gather_fusion.3
  108.8 4.1 fusion.1
  112.9 0.9 fusion.61
  114.3 2.8 fusion.9
  117.1 4.9 convolution_add_fusion.2
  121.9 53.9 %all-reduce.21.cloned.1.call-done = (f32[128,128]{0,1:T(8,128)}, f32[128,128]{0,1:T(8,128)}) async-done(((f32[128,128]{0,1:T(8,128)}, f32[128,128]{0,1:T(8,128)}), (f32[128,128]{0,1:T(8,128)}, f32[128,128]{0,1:T(8,128)})) %all-reduce.21.cloned.1.call-update) | async-done | bytes 131088 | tf_op jit(solution)/shard_map/psum | solution.py:62
  176.1 2.3 fusion.59
  178.4 2.8 fusion.8
  181.2 4.9 convolution_add_fusion.3
  188.0 110.5 %all-reduce.17.cloned.1.call-done = (f32[128,128]{0,1:T(8,128)}, f32[64,16384]{1,0:T(8,128)}, f32[128,128]{0,1:T(8,128)}) async-done(((f32[128,128]{0,1:T(8,128)}, f32[64,16384]{1,0:T(8,128)}, f32[128,128]{0,1:T(8,128)}), (f32[128,128]{0,1:T(8,128)}, f32[64,16384]{1,0:T(8,128)}, f32[128,128]{0,1:T(8,128)})) %all-reduce.17.cloned.1.call-update) | async-done | bytes 4325392 | tf_op jit(solution)/shard_map/psum | solution.py:61
  298.5 1.1 constant_dynamic-slice_fusion.1
  299.6 0.9 reshape.383
  300.5 55.6 %reduce-scatter.3.cloned.1.call-done = f32[8,16384]{1,0:T(8,128)} async-done(((f32[64,16384]{1,0:T(8,128)}), f32[8,16384]{1,0:T(8,128)}) %reduce-scatter.3.cloned.1.call-update) | async-done | bytes 524304 | tf_op jit(solution)/shard_map/reduce_scatter | solution.py:93
  356.0 1.9 reshape.380
  358.7 11.7 %cholesky.74 = f32[128,128]{1,0:T(8,128)S(1)} custom-call(f32[128,128]{1,0:T(8,128)S(1)} %get-tuple-element.30), custom_call_target="Cholesky" | custom-call | tf_op jit(solution)/shard_map/jit(cholesky)/cholesky | solution.py:10
  371.8 9.8 %custom-call.14 = f32[1,128,128]{1,2,0:T(8,128)S(1)} custom-call(f32[1,128,128]{2,1,0:T(8,128)S(1)} %fusion.24), custom_call_target="InvertDiagBlocksLowerTriangular" | custom-call | tf_op jit(solution)/shard_map/jit(_cho_solve)/triangular_solve | solution.py:11
  381.6 6.9 all-reduce.25.cloned.1.call-done
  388.5 1.7 fusion.41
  390.9 0.8 copy.69
  392.4 11.7 %cholesky.85 = f32[128,128]{1,0:T(8,128)S(1)} custom-call(f32[128,128]{1,0:T(8,128)S(1)} %get-tuple-element.29), custom_call_target="Cholesky" | custom-call | tf_op jit(solution)/shard_map/jit(cholesky)/cholesky | solution.py:10
  405.4 9.8 %custom-call.15 = f32[1,128,128]{1,2,0:T(8,128)S(1)} custom-call(f32[1,128,128]{2,1,0:T(8,128)S(1)} %fusion.25), custom_call_target="InvertDiagBlocksLowerTriangular" | custom-call | tf_op jit(solution)/shard_map/jit(_cho_solve)/triangular_solve | solution.py:11
  416.1 0.8 copy.70
  416.9 1.0 fusion.62
  417.9 1.2 fusion.64
  419.4 11.0 %all-gather.9.cloned.1.call-done = bf16[64,128,128]{2,1,0:T(8,128)(2,1)} async-done(((bf16[8,128,128]{2,1,0:T(8,128)(2,1)}), bf16[64,128,128]{2,1,0:T(8,128)(2,1)}) %all-gather.9.cloned.1.call-update) | async-done | bytes 2097168 | tf_op jit(solution)/shard_map/all_gather | solution.py:83
  430.3 3.8 gather_fusion.4
  434.1 50.7 %all-gather.11.cloned.1.call-done = bf16[64,128,128]{2,1,0:T(8,128)(2,1)} async-done(((bf16[4,128,128]{2,1,0:T(8,128)(2,1)}), bf16[64,128,128]{2,1,0:T(8,128)(2,1)}) %all-gather.11.cloned.1.call-update) | async-done | bytes 2097168 | tf_op jit(solution)/shard_map/all_gather | solution.py:84
  484.8 2.5 gather_fusion.5
  487.3 4.1 fusion.3
  491.5 0.9 fusion.65
  492.9 2.8 fusion.11
  495.6 4.9 convolution_add_fusion
  500.5 54.0 %all-reduce.19.cloned.1.call-done = (f32[128,128]{0,1:T(8,128)}, f32[128,128]{0,1:T(8,128)}) async-done(((f32[128,128]{0,1:T(8,128)}, f32[128,128]{0,1:T(8,128)}), (f32[128,128]{0,1:T(8,128)}, f32[128,128]{0,1:T(8,128)})) %all-reduce.19.cloned.1.call-update) | async-done | bytes 131088 | tf_op jit(solution)/shard_map/psum | solution.py:62
  554.5 2.3 fusion.63
  556.8 2.8 fusion.10
  559.6 4.9 convolution_add_fusion.1
  564.8 111.9 %all-reduce.15.cloned.1.call-done = (f32[128,128]{0,1:T(8,128)}, f32[64,16384]{1,0:T(8,128)}, f32[128,128]{0,1:T(8,128)}) async-done(((f32[128,128]{0,1:T(8,128)}, f32[64,16384]{1,0:T(8,128)}, f32[128,128]{0,1:T(8,128)}), (f32[128,128]{0,1:T(8,128)}, f32[64,16384]{1,0:T(8,128)}, f32[128,128]{0,1:T(8,128)})) %all-reduce.15.cloned.1.call-update) | async-done | bytes 4325392 | tf_op jit(solution)/shard_map/psum | solution.py:61
  676.7 1.1 constant_dynamic-slice_fusion
  677.8 0.9 reshape.389
  678.7 0.9 copy.55
  679.6 0.9 fusion.35
  680.5 11.7 %cholesky.96 = f32[128,128]{1,0:T(8,128)S(1)} custom-call(f32[128,128]{1,0:T(8,128)S(1)} %fusion.35), custom_call_target="Cholesky" | custom-call | tf_op jit(solution)/shard_map/jit(cholesky)/cholesky | solution.py:10
  692.9 41.8 %reduce-scatter.5.cloned.1.call-done = f32[8,16384]{1,0:T(8,128)} async-done(((f32[64,16384]{1,0:T(8,128)}), f32[8,16384]{1,0:T(8,128)}) %reduce-scatter.5.cloned.1.call-update) | async-done | bytes 524304 | tf_op jit(solution)/shard_map/reduce_scatter | solution.py:93
  734.7 1.9 reshape.387
  737.3 9.8 %custom-call.16 = f32[1,128,128]{1,2,0:T(8,128)S(1)} custom-call(f32[1,128,128]{2,1,0:T(8,128)S(1)} %fusion.26), custom_call_target="InvertDiagBlocksLowerTriangular" | custom-call | tf_op jit(solution)/shard_map/jit(_cho_solve)/triangular_solve | solution.py:11
  747.2 11.7 %cholesky.107 = f32[128,128]{1,0:T(8,128)S(1)} custom-call(f32[128,128]{1,0:T(8,128)S(1)} %fusion.31), custom_call_target="Cholesky" | custom-call | tf_op jit(solution)/shard_map/jit(cholesky)/cholesky | solution.py:10
  760.3 10.0 %custom-call.17 = f32[1,128,128]{1,2,0:T(8,128)S(1)} custom-call(f32[1,128,128]{2,1,0:T(8,128)S(1)} %fusion.27), custom_call_target="InvertDiagBlocksLowerTriangular" | custom-call | tf_op jit(solution)/shard_map/jit(_cho_solve)/triangular_solve | solution.py:11
  770.4 1.7 fusion.33
  772.7 1.0 copy.61
  774.5 0.8 copy.62
  (101 shorter events, 15.9 us)
Async XLA Ops:
  7.2 14.9 %copy-start.4 = (f32[1024,128]{1,0:T(8,128)S(1)}, f32[1024,128]{1,0:T(8,128)}, u32[]{:S(2)}) copy-start(f32[1024,128]{1,0:T(8,128)} %param.14) | copy-start | bytes 1572868
  7.2 16.5 %copy-start.15 = (s32[1,1,1,64]{3,2,1,0:T(1,128)S(1)}, s32[1,1,1,64]{3,2,1,0:T(1,128)}, u32[]{:S(2)}) copy-start(s32[1,1,1,64]{3,2,1,0:T(1,128)} %param.19) | copy-start | bytes 772
  7.2 16.6 %copy-start.14 = (s32[1,1,1,64]{3,2,1,0:T(1,128)S(1)}, s32[1,1,1,64]{3,2,1,0:T(1,128)}, u32[]{:S(2)}) copy-start(s32[1,1,1,64]{3,2,1,0:T(1,128)} %param.20) | copy-start | bytes 772
  7.2 16.6 %copy-start.13 = (s32[1,1,1,8,4]{3,4,2,1,0:T(4,128)S(1)}, s32[1,1,1,8,4]{3,4,2,1,0:T(4,128)}, u32[]{:S(2)}) copy-start(s32[1,1,1,8,4]{3,4,2,1,0:T(4,128)} %param.21) | copy-start | bytes 388
  7.2 44.5 %all-gather.5.cloned.1.call-start = ((), (), s32[]{:S(2)}) async-start(), calls=%async_computation.4 | async-start | bytes 2359296 | tf_op jit(solution)/shard_map/all_gather | solution.py:83
  9.1 97.1 %all-gather.7.cloned.1.call-start = ((), (), s32[]{:S(2)}) async-start(), calls=%async_computation.5 | async-start | bytes 2228224 | tf_op jit(solution)/shard_map/all_gather | solution.py:84
  12.1 14.0 %all-to-all-start.1 = ((s32[16,1,2]{2,1,0:T(1,128)}), s32[16,1,2]{2,1,0:T(1,128)S(1)}, u32[]{:S(2)}, u32[]{:S(2)}) async-start(s32[16,1,2]{2,1,0:T(1,128)} %copy.48), calls=%async_computation.1 | async-start | bytes 16384 | tf_op jit(solution)/shard_map/all_to_all | solution.py:51
  19.7 156.1 %all-reduce.21.cloned.1.call-start = ((), (), s32[]{:S(2)}) async-start(), calls=%async_computation.13 | async-start | bytes 262144 | tf_op jit(solution)/shard_map/psum | solution.py:62
  26.1 14.8 %all-to-all-start = ((s32[8,1,4]{2,1,0:T(1,128)}), s32[8,1,4]{2,1,0:T(1,128)S(1)}, u32[]{:S(2)}, u32[]{:S(2)}) async-start(s32[8,1,4]{2,1,0:T(1,128)} %copy.47), calls=%async_computation | async-start | bytes 8192 | tf_op jit(solution)/shard_map/all_to_all | solution.py:48
  34.3 264.1 %all-reduce.17.cloned.1.call-start = ((), (), s32[]{:S(2)}) async-start(), calls=%async_computation.11 | async-start | bytes 8650752 | tf_op jit(solution)/shard_map/psum | solution.py:61
  55.5 53.3 %copy-start.11 = (s32[1,1,1,64,128]{4,3,2,1,0:T(8,128)S(1)}, s32[1,1,1,64,128]{4,3,2,1,0:T(8,128)}, u32[]{:S(2)}) copy-start(s32[1,1,1,64,128]{4,3,2,1,0:T(8,128)} %param.18) | copy-start | bytes 98308
  55.5 53.3 %copy-start.12 = (s32[1,1,1,64,128]{4,3,2,1,0:T(8,128)S(1)}, s32[1,1,1,64,128]{4,3,2,1,0:T(8,128)}, u32[]{:S(2)}) copy-start(s32[1,1,1,64,128]{4,3,2,1,0:T(8,128)} %param.17) | copy-start | bytes 98308
  108.8 4.1 copy-start.1
  112.9 1.4 copy-start.2
  175.8 180.2 %reduce-scatter.3.cloned.1.call-start = ((), (), s32[]{:S(2)}) async-start(), calls=%async_computation.6 | async-start | bytes 4718592 | tf_op jit(solution)/shard_map/reduce_scatter | solution.py:93
  186.0 0.7 copy-start.16
  186.1 202.5 %all-reduce.25.cloned.1.call-start = ((), (), s32[]{:S(2)}) async-start(), calls=%async_computation.15 | async-start | bytes 1572864 | tf_op jit(solution)/shard_map/psum | solution.py:95
  298.4 60.0 %copy-start.10 = (f32[128,128]{0,1:T(8,128)S(1)}, f32[128,128]{0,1:T(8,128)}, u32[]{:S(2)}) copy-start(f32[128,128]{0,1:T(8,128)} %get-tuple-element.16) | copy-start | bytes 196612
  298.4 60.1 %copy-start.9 = (f32[128,128]{0,1:T(8,128)S(1)}, f32[128,128]{0,1:T(8,128)}, u32[]{:S(2)}) copy-start(f32[128,128]{0,1:T(8,128)} %get-tuple-element.14) | copy-start | bytes 196612
  358.0 72.4 %all-gather.9.cloned.1.call-start = ((), (), s32[]{:S(2)}) async-start(), calls=%async_computation.7 | async-start | bytes 2359296 | tf_op jit(solution)/shard_map/all_gather | solution.py:83
  358.7 33.5 %copy-start.5 = (f32[512,128]{1,0:T(8,128)S(1)}, f32[512,128]{1,0:T(8,128)}, u32[]{:S(2)}) copy-start(f32[512,128]{1,0:T(8,128)} %param.15) | copy-start | bytes 786436
  388.5 26.7 %copy-start.7 = (f32[128,512]{0,1:T(8,128)S(1)}, f32[128,512]{0,1:T(8,128)}, u32[]{:S(2)}) copy-start(f32[128,512]{0,1:T(8,128)} %get-tuple-element.24) | copy-start | bytes 786436
  391.7 93.0 %all-gather.11.cloned.1.call-start = ((), (), s32[]{:S(2)}) async-start(), calls=%async_computation.8 | async-start | bytes 2228224 | tf_op jit(solution)/shard_map/all_gather | solution.py:84
  416.9 137.6 %all-reduce.19.cloned.1.call-start = ((), (), s32[]{:S(2)}) async-start(), calls=%async_computation.12 | async-start | bytes 262144 | tf_op jit(solution)/shard_map/psum | solution.py:62
  419.1 257.6 %all-reduce.15.cloned.1.call-start = ((), (), s32[]{:S(2)}) async-start(), calls=%async_computation.10 | async-start | bytes 8650752 | tf_op jit(solution)/shard_map/psum | solution.py:61
  487.3 4.1 copy-start
  491.5 1.4 copy-start.3
  554.5 180.2 %reduce-scatter.5.cloned.1.call-start = ((), (), s32[]{:S(2)}) async-start(), calls=%async_computation.9 | async-start | bytes 4718592 | tf_op jit(solution)/shard_map/reduce_scatter | solution.py:93
  564.5 205.9 %all-reduce.23.cloned.1.call-start = ((), (), s32[]{:S(2)}) async-start(), calls=%async_computation.14 | async-start | bytes 1572864 | tf_op jit(solution)/shard_map/psum | solution.py:95
  676.7 70.4 %copy-start.6 = (f32[128,128]{0,1:T(8,128)S(1)}, f32[128,128]{0,1:T(8,128)}, u32[]{:S(2)}) copy-start(f32[128,128]{0,1:T(8,128)} %get-tuple-element.13) | copy-start | bytes 196612
  770.4 3.3 copy-start.8
Sparse Core Ops, SparseCore 0:
  10.4 41.2 all-gather.4
  54.7 51.4 all-gather.6
  108.5 67.2 all-reduce.20
  179.7 118.6 all-reduce.16
  300.8 55.1 reduce-scatter.2
  359.1 29.3 all-reduce.24
  391.8 38.4 all-gather.8
  433.6 51.1 all-gather.10
  487.2 67.1 all-reduce.18
  558.0 118.6 all-reduce.14
  679.4 55.2 reduce-scatter.4
  738.0 29.5 all-reduce.22
